TPU v7x, 32 devices: a whole 2x2x4 slice. The times are simulated.
32 devices in a mesh: shard: 4 (over y, x), rep: 8 (over z, core).
Axes of the slice: x: 2, y: 2, z: 4, core: 2. Of those that a mesh axis runs over, the one named last changes fastest.
Arguments:
- tokens: bfloat16 [32768, 1024], P(('shard', 'rep')), may hold values from -6 to 6
- cotangent: bfloat16 [32768, 1024], P(('shard', 'rep')), may hold values from -6 to 6
- segment: int32 [32768], P(('shard', 'rep')), may hold values from -1 to 15, as said below
- attn_gain: bfloat16 [1024], P('shard'), may hold values from 0.5 to 1.5
- w_query: bfloat16 [1024, 1024], P('shard'), may hold values from -0.1875 to 0.1875
- w_key: bfloat16 [1024, 512], P('shard'), may hold values from -0.1875 to 0.1875
- w_value: bfloat16 [1024, 512], P('shard'), may hold values from -0.1875 to 0.1875
- qk_gain: bfloat16 [128], P('shard'), may hold values from 0.099609375 to 1.8984375
- w_out: bfloat16 [1024, 1024], P('shard'), may hold values from -1.5 to 1.5
- ffn_gain: bfloat16 [1024], P('shard'), may hold values from 0.5 to 1.5
- w_gate: bfloat16 [1024, 4608], P('shard'), may hold values from -0.1875 to 0.1875
- w_up: bfloat16 [1024, 4608], P('shard'), may hold values from -0.1875 to 0.1875
- w_down: bfloat16 [4608, 1024], P('shard'), may hold values from -0.09375 to 0.09375
Outputs:
- out: bfloat16 [32768, 1024], P(('shard', 'rep'))
- grad_tokens: bfloat16 [32768, 1024], P(('shard', 'rep'))
- grad_attn_gain: float32 [1024], P('shard')
- grad_w_query: float32 [1024, 1024], P('shard')
- grad_w_key: float32 [1024, 512], P('shard')
- grad_w_value: float32 [1024, 512], P('shard')
- grad_qk_gain: float32 [128], P('shard')
- grad_w_out: float32 [1024, 1024], P('shard')
- grad_ffn_gain: float32 [1024], P('shard')
- grad_w_gate: float32 [1024, 4608], P('shard')
- grad_w_up: float32 [1024, 4608], P('shard')
- grad_w_down: float32 [4608, 1024], P('shard')
Inputs may be any that keep to these rules, and one draw needn't show every extreme that they name: `segment`: within each device's 1024 slots the live tokens come first, 512 to 1024 of them, followed by padding marked -1; live tokens form runs of equal ids 0, 1, 2, ... in rising order, each run one sequence of 1 to 512 tokens, at most 16 of them on a device. Some device has no padding and holds 16 sequences, some has 512 live tokens, and some sequence has exactly 512 tokens.
All inputs are finite; a program needn't handle non-finite values.
Results may differ from a plain program's by a relative error of at most 0.02.
Values may be sent and summed in bfloat16 or wider, within the bound.
No kernel may reach another device: no remote copies, remote signals or barrier semaphores. Data moves between devices by JAX's collectives and lax.ppermute only.
A program may use at most 384 MiB of HBM per device.

v0:
```python
import math
import jax
import jax.numpy as jnp
from jax import lax
from jax.sharding import PartitionSpec as P

HQ = 16
HK = 8
HD = 64
norm_eps = 1e-05
rope_base = 1000000.0


def inv_rms(values):
    return lax.rsqrt(jnp.mean(values * values, axis=-1, keepdims=True) + norm_eps)


def rope_tables(positions):
    half_dim = HD // 2
    freq_index = jnp.arange(half_dim).astype(jnp.float32)
    freq_vals = jnp.power(rope_base, -(2.0 * freq_index) / HD)
    angles = positions[:, None] * freq_vals[None, :]
    return (jnp.cos(angles)[:, None, :], jnp.sin(angles)[:, None, :])


def rotate(values, cosine, sine_table):
    half_dim = HD // 2
    first_half = values[..., :half_dim]
    second_half = values[..., half_dim:]
    return jnp.concatenate(
        [
            first_half * cosine - second_half * sine_table,
            second_half * cosine + first_half * sine_table,
        ],
        axis=-1,
    )


def rotate_back(grad_vals, cosine, sine_table):
    half_dim = HD // 2
    first_half = grad_vals[..., :half_dim]
    second_half = grad_vals[..., half_dim:]
    return jnp.concatenate(
        [
            first_half * cosine + second_half * sine_table,
            second_half * cosine - first_half * sine_table,
        ],
        axis=-1,
    )


def norm_back(grad_out, inputs, scale_inv, gain_vec):
    weighted = grad_out * gain_vec
    row_inner = jnp.mean(weighted * inputs, axis=-1, keepdims=True)
    return scale_inv * weighted - inputs * (scale_inv * scale_inv * scale_inv) * row_inner


def matmul_plain(left_mat, right_mat):
    return jnp.dot(left_mat, right_mat, preferred_element_type=jnp.float32)


def matmul_rows(left_mat, right_mat):
    return lax.dot_general(
        left_mat, right_mat, (((0,), (0,)), ((), ())), preferred_element_type=jnp.float32
    )


def matmul_cols(left_mat, right_mat):
    return lax.dot_general(
        left_mat, right_mat, (((1,), (1,)), ((), ())), preferred_element_type=jnp.float32
    )


def body(
    tokens,
    cotangent,
    segment,
    attn_gain,
    w_query,
    w_key,
    w_value,
    qk_gain,
    w_out,
    ffn_gain,
    w_gate,
    w_up,
    w_down,
):
    row_count = tokens.shape[0]
    group_size = HQ // HK
    score_scale = 1.0 / math.sqrt(HD)
    block_rows = min(512, row_count)
    block_count = row_count // block_rows
    attn_set = (
        lax.all_gather(attn_gain, "shard", axis=0, tiled=True),
        lax.all_gather(w_query, "shard", axis=0, tiled=True),
        lax.all_gather(w_key, "shard", axis=0, tiled=True),
        lax.all_gather(w_value, "shard", axis=0, tiled=True),
        lax.all_gather(qk_gain, "shard", axis=0, tiled=True),
        lax.all_gather(w_out, "shard", axis=0, tiled=True),
    )
    full_attn_gain, full_query, full_key, full_value, full_qk_gain, full_out = attn_set
    inputs = tokens.astype(jnp.float32)
    token_index = jnp.arange(row_count)
    same_seq = segment[:, None] == segment[None, :]
    allowed = same_seq & (token_index[None, :] <= token_index[:, None])
    positions = jnp.sum(
        (same_seq & (token_index[None, :] < token_index[:, None])).astype(jnp.float32), axis=1
    )
    live_rows = (segment >= 0).astype(jnp.float32)[:, None]
    cosine, sine_table = rope_tables(positions)
    scale_one = inv_rms(inputs)
    normed = (inputs * scale_one * full_attn_gain.astype(jnp.float32)).astype(jnp.bfloat16)
    query_lin = matmul_plain(normed, full_query).reshape(row_count, HQ, HD)
    key_lin = matmul_plain(normed, full_key).reshape(row_count, HK, HD)
    value_low = matmul_plain(normed, full_value).astype(jnp.bfloat16).reshape(row_count, HK, HD)
    qk_gains = full_qk_gain.astype(jnp.float32)
    query_scale = inv_rms(query_lin)
    key_scale = inv_rms(key_lin)
    query_rot = (
        rotate(query_lin * query_scale * qk_gains[:HD], cosine, sine_table)
        .astype(jnp.bfloat16)
        .reshape(row_count, HK, group_size, HD)
    )
    key_rot = rotate(key_lin * key_scale * qk_gains[HD:], cosine, sine_table).astype(jnp.bfloat16)

    def block_scores(begin_row):
        query_block = query_rot[begin_row : begin_row + block_rows]
        raw_scores = score_scale * jnp.einsum(
            "qgrd,kgd->grqk", query_block, key_rot, preferred_element_type=jnp.float32
        )
        mask_block = allowed[begin_row : begin_row + block_rows]
        return jnp.where(mask_block[None, None, :, :], raw_scores, -1e30)

    lse_parts = []
    attended_parts = []
    for block_id in range(block_count):
        begin_row = block_id * block_rows
        masked = block_scores(begin_row)
        row_peak = jnp.max(masked, axis=-1, keepdims=True)
        exp_scores = jnp.exp(masked - row_peak)
        row_total = jnp.sum(exp_scores, axis=-1, keepdims=True)
        probs_low = (exp_scores / row_total).astype(jnp.bfloat16)
        lse_parts.append(row_peak + jnp.log(row_total))
        attended_parts.append(
            jnp.einsum("grqk,kgd->qgrd", probs_low, value_low, preferred_element_type=jnp.float32)
        )
    attn_low = (
        jnp.concatenate(attended_parts, axis=0).astype(jnp.bfloat16).reshape(row_count, HQ * HD)
    )
    hidden = inputs + matmul_plain(attn_low, full_out)
    ffn_set = (
        lax.all_gather(ffn_gain, "shard", axis=0, tiled=True),
        lax.all_gather(w_gate, "shard", axis=0, tiled=True),
        lax.all_gather(w_up, "shard", axis=0, tiled=True),
        lax.all_gather(w_down, "shard", axis=0, tiled=True),
    )
    full_ffn_gain, full_gate, full_up, full_down = ffn_set
    scale_two = inv_rms(hidden)
    normed_ffn = (hidden * scale_two * full_ffn_gain.astype(jnp.float32)).astype(jnp.bfloat16)
    gate_proj = matmul_plain(normed_ffn, full_gate)
    up_proj = matmul_plain(normed_ffn, full_up)
    gate_sig = jax.nn.sigmoid(gate_proj)
    gate_act = gate_proj * gate_sig
    mixed_act = (gate_act * up_proj).astype(jnp.bfloat16)
    result = live_rows * (hidden + matmul_plain(mixed_act, full_down))
    back_ffn = (
        lax.all_gather(ffn_gain, "shard", axis=0, tiled=True),
        lax.all_gather(w_gate, "shard", axis=0, tiled=True),
        lax.all_gather(w_up, "shard", axis=0, tiled=True),
        lax.all_gather(w_down, "shard", axis=0, tiled=True),
    )
    back_ffn_gain, back_gate, back_up, back_down = back_ffn
    out_grad = live_rows * cotangent.astype(jnp.float32)
    out_low = out_grad.astype(jnp.bfloat16)
    grad_mixed = matmul_cols(out_low, back_down)
    grad_w_down = matmul_rows(mixed_act, out_low)
    grad_up_low = (grad_mixed * gate_act).astype(jnp.bfloat16)
    grad_gate_low = (grad_mixed * up_proj * gate_sig * (1.0 + gate_proj * (1.0 - gate_sig))).astype(
        jnp.bfloat16
    )
    grad_w_gate = matmul_rows(normed_ffn, grad_gate_low)
    grad_w_up = matmul_rows(normed_ffn, grad_up_low)
    grad_normed_ffn = matmul_cols(grad_gate_low, back_gate) + matmul_cols(grad_up_low, back_up)
    grad_ffn_gain = jnp.sum(grad_normed_ffn * hidden * scale_two, axis=0)
    grad_hidden = out_grad + norm_back(
        grad_normed_ffn, hidden, scale_two, back_ffn_gain.astype(jnp.float32)
    )
    share_fgain, share_gate, share_up, share_down = (
        lax.psum_scatter(
            grad_ffn_gain.astype(jnp.bfloat16), "shard", scatter_dimension=0, tiled=True
        ).astype(jnp.float32),
        lax.psum_scatter(
            grad_w_gate.astype(jnp.bfloat16), "shard", scatter_dimension=0, tiled=True
        ).astype(jnp.float32),
        lax.psum_scatter(
            grad_w_up.astype(jnp.bfloat16), "shard", scatter_dimension=0, tiled=True
        ).astype(jnp.float32),
        lax.psum_scatter(
            grad_w_down.astype(jnp.bfloat16), "shard", scatter_dimension=0, tiled=True
        ).astype(jnp.float32),
    )
    back_attn = (
        lax.all_gather(attn_gain, "shard", axis=0, tiled=True),
        lax.all_gather(w_query, "shard", axis=0, tiled=True),
        lax.all_gather(w_key, "shard", axis=0, tiled=True),
        lax.all_gather(w_value, "shard", axis=0, tiled=True),
        lax.all_gather(qk_gain, "shard", axis=0, tiled=True),
        lax.all_gather(w_out, "shard", axis=0, tiled=True),
    )
    back_attn_gain, back_query, back_key, back_value, back_qk_gain, back_out = back_attn
    hidden_low = grad_hidden.astype(jnp.bfloat16)
    grad_attn_low = (
        matmul_cols(hidden_low, back_out)
        .astype(jnp.bfloat16)
        .reshape(row_count, HK, group_size, HD)
    )
    grad_w_out = matmul_rows(attn_low, hidden_low)
    grad_query_parts = []
    grad_key_rot = jnp.zeros((row_count, HK, HD), jnp.float32)
    grad_value = jnp.zeros((row_count, HK, HD), jnp.float32)
    for block_id in range(block_count):
        begin_row = block_id * block_rows
        masked = block_scores(begin_row)
        attn_probs = jnp.exp(masked - lse_parts[block_id])
        probs_low = attn_probs.astype(jnp.bfloat16)
        grad_block = grad_attn_low[begin_row : begin_row + block_rows]
        query_block = query_rot[begin_row : begin_row + block_rows]
        grad_probs = jnp.einsum(
            "qgrd,kgd->grqk", grad_block, value_low, preferred_element_type=jnp.float32
        )
        row_inner = jnp.sum(attn_probs * grad_probs, axis=-1, keepdims=True)
        grad_scores = (attn_probs * (grad_probs - row_inner)).astype(jnp.bfloat16)
        grad_query_parts.append(
            score_scale
            * jnp.einsum("grqk,kgd->qgrd", grad_scores, key_rot, preferred_element_type=jnp.float32)
        )
        grad_key_rot = grad_key_rot + score_scale * jnp.einsum(
            "grqk,qgrd->kgd", grad_scores, query_block, preferred_element_type=jnp.float32
        )
        grad_value = grad_value + jnp.einsum(
            "grqk,qgrd->kgd", probs_low, grad_block, preferred_element_type=jnp.float32
        )
    grad_query_rot = jnp.concatenate(grad_query_parts, axis=0).reshape(row_count, HQ, HD)
    grad_query_norm = rotate_back(grad_query_rot, cosine, sine_table)
    grad_key_norm = rotate_back(grad_key_rot, cosine, sine_table)
    back_gains = back_qk_gain.astype(jnp.float32)
    grad_qk_gain = jnp.concatenate(
        [
            jnp.sum(grad_query_norm * query_lin * query_scale, axis=(0, 1)),
            jnp.sum(grad_key_norm * key_lin * key_scale, axis=(0, 1)),
        ]
    )
    grad_query_low = (
        norm_back(grad_query_norm, query_lin, query_scale, back_gains[:HD])
        .astype(jnp.bfloat16)
        .reshape(row_count, HQ * HD)
    )
    grad_key_low = (
        norm_back(grad_key_norm, key_lin, key_scale, back_gains[HD:])
        .astype(jnp.bfloat16)
        .reshape(row_count, HK * HD)
    )
    grad_value_low = grad_value.astype(jnp.bfloat16).reshape(row_count, HK * HD)
    grad_w_query = matmul_rows(normed, grad_query_low)
    grad_w_key = matmul_rows(normed, grad_key_low)
    grad_w_value = matmul_rows(normed, grad_value_low)
    grad_normed = (
        matmul_cols(grad_query_low, back_query)
        + matmul_cols(grad_key_low, back_key)
        + matmul_cols(grad_value_low, back_value)
    )
    grad_attn_gain = jnp.sum(grad_normed * inputs * scale_one, axis=0)
    grad_inputs = grad_hidden + norm_back(
        grad_normed, inputs, scale_one, back_attn_gain.astype(jnp.float32)
    )
    share_again, share_query, share_key, share_value, share_qk, share_out = (
        lax.psum_scatter(
            grad_attn_gain.astype(jnp.bfloat16), "shard", scatter_dimension=0, tiled=True
        ).astype(jnp.float32),
        lax.psum_scatter(
            grad_w_query.astype(jnp.bfloat16), "shard", scatter_dimension=0, tiled=True
        ).astype(jnp.float32),
        lax.psum_scatter(
            grad_w_key.astype(jnp.bfloat16), "shard", scatter_dimension=0, tiled=True
        ).astype(jnp.float32),
        lax.psum_scatter(
            grad_w_value.astype(jnp.bfloat16), "shard", scatter_dimension=0, tiled=True
        ).astype(jnp.float32),
        lax.psum_scatter(
            grad_qk_gain.astype(jnp.bfloat16), "shard", scatter_dimension=0, tiled=True
        ).astype(jnp.float32),
        lax.psum_scatter(
            grad_w_out.astype(jnp.bfloat16), "shard", scatter_dimension=0, tiled=True
        ).astype(jnp.float32),
    )
    (
        share_again,
        share_query,
        share_key,
        share_value,
        share_qk,
        share_out,
        share_fgain,
        share_gate,
        share_up,
        share_down,
    ) = (
        lax.psum(share_again.astype(jnp.bfloat16), "rep").astype(jnp.float32),
        lax.psum(share_query.astype(jnp.bfloat16), "rep").astype(jnp.float32),
        lax.psum(share_key.astype(jnp.bfloat16), "rep").astype(jnp.float32),
        lax.psum(share_value.astype(jnp.bfloat16), "rep").astype(jnp.float32),
        lax.psum(share_qk.astype(jnp.bfloat16), "rep").astype(jnp.float32),
        lax.psum(share_out.astype(jnp.bfloat16), "rep").astype(jnp.float32),
        lax.psum(share_fgain.astype(jnp.bfloat16), "rep").astype(jnp.float32),
        lax.psum(share_gate.astype(jnp.bfloat16), "rep").astype(jnp.float32),
        lax.psum(share_up.astype(jnp.bfloat16), "rep").astype(jnp.float32),
        lax.psum(share_down.astype(jnp.bfloat16), "rep").astype(jnp.float32),
    )
    return (
        result.astype(jnp.bfloat16),
        grad_inputs.astype(jnp.bfloat16),
        share_again,
        share_query,
        share_key,
        share_value,
        share_qk,
        share_out,
        share_fgain,
        share_gate,
        share_up,
        share_down,
    )


def solution(mesh):
    return jax.shard_map(
        body,
        mesh=mesh,
        in_specs=(
            P(("shard", "rep"), None),
            P(("shard", "rep"), None),
            P(("shard", "rep")),
            P("shard"),
            P("shard", None),
            P("shard", None),
            P("shard", None),
            P("shard"),
            P("shard", None),
            P("shard"),
            P("shard", None),
            P("shard", None),
            P("shard", None),
        ),
        out_specs=(
            P(("shard", "rep"), None),
            P(("shard", "rep"), None),
            P("shard"),
            P("shard", None),
            P("shard", None),
            P("shard", None),
            P("shard"),
            P("shard", None),
            P("shard"),
            P("shard", None),
            P("shard", None),
            P("shard", None),
        ),
        check_vma=False,
    )
```

profile of v0, /device:TPU:0, one launch (start us, length us, event | category | flops | bytes accessed | tf_op | source)
XLA Modules:
  0.0 1275.4 jit_solution(9859009708675031357)
XLA Ops:
  71.4 33.6 %all-gather.14.cloned.1.call-done = bf16[1024,1024]{1,0:T(8,128)(2,1)} async-done(((bf16[256,1024]{1,0:T(8,128)(2,1)}), bf16[1024,1024]{1,0:T(8,128)(2,1)}) %all-gather.14.cloned.1.call-update) | async-done | bytes 2097168 | tf_op jit(solution)/shard_map/all_gather | solution.py:96
  112.6 13.6 %fusion.63 = (f32[8,2,512]{2,1,0:T(2,128)S(1)}, f32[8,2,512,1024]{2,3,1,0:T(8,128)}) fusion(bf16[512,8,2,64]{0,3,2,1:T(8,128)(2,1)S(1)} %bitcast.196, bf16[1024,8,32]{0,2,1:T(8,128)(2,1)S(1)} %get-tuple-element.81, bf16[1024,8,32]{0,2,1:T(8,128)(2,1)S(1)} %get-tuple-element.80, pred[512,1024]{0,1:T(8,128)(4,1)S(1)} %copy-done.21), kind=kOutput, calls=%fused_computation.153 | convolution fusion | flops 1100996608 | bytes 36208640 | tf_op jit(solution)/shard_map/qgrd,kgd->grqk/dot_general | solution.py:129
  126.2 13.7 %fusion.7 = f32[8,2,512]{2,1,0:T(2,128)S(1)} fusion(f32[8,2,512,1024]{2,3,1,0:T(8,128)} %get-tuple-element.109, f32[8,2,512]{2,1,0:T(2,128)S(1)} %get-tuple-element.108), kind=kLoop, calls=%fused_computation.19 | loop fusion | flops 16769024 | bytes 33619968 | tf_op jit(solution)/shard_map/reduce_sum | solution.py:142
  139.9 14.9 %fusion.44 = bf16[8,64,2,512]{3,1,2,0:T(8,128)(2,1)} fusion(bf16[1024,8,64,1]{0,2,3,1:T(8,128)(2,1)S(1)} %bitcast.200, f32[8,2,512,1024]{2,3,1,0:T(8,128)} %get-tuple-element.109, f32[8,2,512]{2,1,0:T(2,128)S(1)} %fusion.7, f32[8,2,512]{2,1,0:T(2,128)S(1)} %get-tuple-element.108), kind=kOutput, calls=%fused_computation.115 | convolution fusion | flops 1099431936 | bytes 35717120 | tf_op jit(solution)/shard_map/grqk,kgd->qgrd/dot_general | solution.py:146
  154.8 13.5 %fusion.64 = (f32[8,2,512]{2,1,0:T(2,128)S(1)}, f32[8,2,512,1024]{2,3,1,0:T(8,128)}) fusion(bf16[512,8,2,64]{0,3,2,1:T(8,128)(2,1)S(1)} %bitcast.194, bf16[1024,8,32]{0,2,1:T(8,128)(2,1)S(1)} %get-tuple-element.81, bf16[1024,8,32]{0,2,1:T(8,128)(2,1)S(1)} %get-tuple-element.80, pred[512,1024]{0,1:T(8,128)(4,1)S(1)} %copy-done.20), kind=kOutput, calls=%fused_computation.154 | convolution fusion | flops 1100996608 | bytes 36208640 | tf_op jit(solution)/shard_map/qgrd,kgd->grqk/dot_general | solution.py:129
  168.3 13.1 %fusion.6 = f32[8,2,512]{2,1,0:T(2,128)S(1)} fusion(f32[8,2,512,1024]{2,3,1,0:T(8,128)} %get-tuple-element.111, f32[8,2,512]{2,1,0:T(2,128)S(1)} %get-tuple-element.110), kind=kLoop, calls=%fused_computation.18 | loop fusion | flops 16769024 | bytes 33619968 | tf_op jit(solution)/shard_map/reduce_sum | solution.py:142
  181.5 16.7 %fusion.45 = bf16[8,64,2,512]{3,1,2,0:T(8,128)(2,1)} fusion(bf16[1024,8,64,1]{0,2,3,1:T(8,128)(2,1)S(1)} %bitcast.201, f32[8,2,512,1024]{2,3,1,0:T(8,128)} %get-tuple-element.111, f32[8,2,512]{2,1,0:T(2,128)S(1)} %fusion.6, f32[8,2,512]{2,1,0:T(2,128)S(1)} %get-tuple-element.110), kind=kOutput, calls=%fused_computation.116 | convolution fusion | flops 1099431936 | bytes 35717120 | tf_op jit(solution)/shard_map/grqk,kgd->qgrd/dot_general | solution.py:146
  205.5 34.6 %all-gather.20.cloned.1.call-done = bf16[1024,4608]{1,0:T(8,128)(2,1)} async-done(((bf16[256,4608]{1,0:T(8,128)(2,1)}), bf16[1024,4608]{1,0:T(8,128)(2,1)}) %all-gather.20.cloned.1.call-update) | async-done | bytes 9437200 | tf_op jit(solution)/shard_map/all_gather | solution.py:155
  240.1 16.2 %fusion.66 = f32[1024,4608]{1,0:T(8,128)} fusion(bf16[1024,1024]{0,1:T(8,128)(2,1)S(1)} %multiply_convert_fusion.4, bf16[1024,4608]{1,0:T(8,128)(2,1)} %all-gather.20.cloned.1.call-done), kind=kOutput, calls=%fused_computation.156 | convolution fusion | flops 9663676416 | bytes 30408704 | tf_op jit(solution)/shard_map/dot_general | solution.py:59
  256.3 81.8 %all-gather.18.cloned.1.call-done = bf16[1024,4608]{1,0:T(8,128)(2,1)} async-done(((bf16[256,4608]{1,0:T(8,128)(2,1)}), bf16[1024,4608]{1,0:T(8,128)(2,1)}) %all-gather.18.cloned.1.call-update) | async-done | bytes 9437200 | tf_op jit(solution)/shard_map/all_gather | solution.py:154
  338.2 17.1 %fusion.65 = f32[1024,4608]{1,0:T(8,128)} fusion(bf16[1024,1024]{0,1:T(8,128)(2,1)} %copy-done.31, bf16[1024,4608]{1,0:T(8,128)(2,1)} %all-gather.18.cloned.1.call-done), kind=kOutput, calls=%fused_computation.155 | convolution fusion | flops 9663676416 | bytes 30408704 | tf_op jit(solution)/shard_map/dot_general | solution.py:59
  355.2 81.1 %all-gather.22.cloned.1.call-done = bf16[4608,1024]{1,0:T(8,128)(2,1)} async-done(((bf16[1152,1024]{1,0:T(8,128)(2,1)}), bf16[4608,1024]{1,0:T(8,128)(2,1)}) %all-gather.22.cloned.1.call-update) | async-done | bytes 9437200 | tf_op jit(solution)/shard_map/all_gather | solution.py:156
  436.4 31.2 %multiply_convert_fusion = (bf16[1024,4608]{1,0:T(8,128)(2,1)}, bf16[1024,4608]{1,0:T(8,128)(2,1)}, bf16[1024,4608]{1,0:T(8,128)(2,1)}) fusion(f32[1024,4608]{1,0:T(8,128)} %fusion.65, f32[1024,4608]{1,0:T(8,128)} %fusion.66, bf16[4608,1024]{1,0:T(8,128)(2,1)} %all-gather.22.cloned.1.call-done, bf16[1024,1024]{0,1:T(8,128)(2,1)S(1)} %copy-done.18, ...), kind=kOutput, calls=%fused_computation.22 | convolution fusion | flops 9737601024 | bytes 77598720 | tf_op jit(solution)/shard_map/dot_general | solution.py:69
  467.6 14.6 %fusion.67 = f32[1024,1024]{0,1:T(8,128)S(1)} fusion(bf16[1024,4608]{1,0:T(8,128)(2,1)} %get-tuple-element.66, bf16[1024,4608]{1,0:T(8,128)(2,1)} %all-gather.18.cloned.1.call-done), kind=kOutput, calls=%fused_computation.157 | convolution fusion | flops 9663676416 | bytes 23068672 | tf_op jit(solution)/shard_map/dot_general | solution.py:69
  482.2 16.5 %multiply_reduce_fusion = (bf16[1024]{0:T(1024)(128)(2,1)}, f32[1024]{0:T(1024)S(1)}, f32[1024,1024]{0,1:T(8,128)S(1)}) fusion(f32[1024,1024]{0,1:T(8,128)S(1)} %copy-done.9, f32[1024]{0:T(1024)S(1)} %get-tuple-element.99, f32[1024]{0:T(1024)S(1)} %bitcast.223, f32[1024,1024]{0,1:T(8,128)S(1)} %fusion.67, bf16[1024,4608]{1,0:T(8,128)(2,1)} %get-tuple-element.65, ...), kind=kOutput, calls=%fused_computation.65 | convolution fusion | flops 9671014400 | bytes 31471616 | tf_op jit(solution)/shard_map/dot_general | solution.py:69
  502.8 14.7 %fusion.11 = f32[8,64,1024,1]{2,1,3,0:T(8,128)} fusion(bf16[512,8,2,64]{0,3,2,1:T(8,128)(2,1)S(1)} %bitcast.192, f32[8,2,512,1024]{2,3,1,0:T(8,128)} %get-tuple-element.109, f32[8,2,512]{2,1,0:T(2,128)S(1)} %bitcast.204), kind=kOutput, calls=%fused_computation.27 | convolution fusion | flops 1090519040 | bytes 36732928 | tf_op jit(solution)/shard_map/grqk,qgrd->kgd/dot_general | solution.py:241
  517.5 21.8 %fusion = (f32[8,2,512]{2,1,0:T(2,128)S(1)}, f32[8,1024,512,2]{2,1,3,0:T(8,128)}) fusion(f32[8,2,512,1024]{2,3,1,0:T(8,128)} %get-tuple-element.109, f32[8,2,512]{2,1,0:T(2,128)S(1)} %bitcast.205, bf16[1024,8,64,1]{0,2,3,1:T(8,128)(2,1)S(1)} %bitcast.202, bf16[512,8,2,64]{0,3,2,1:T(8,128)(2,1)S(1)} %bitcast.193), kind=kOutput, calls=%fused_computation.2 | convolution fusion | flops 1098899456 | bytes 69271552 | tf_op jit(solution)/shard_map/qgrd,kgd->grqk/dot_general | solution.py:229
  539.3 21.7 %fusion.3 = (f32[8,2,512]{2,1,0:T(2,128)S(1)}, f32[8,1024,512,2]{2,1,3,0:T(8,128)}) fusion(f32[8,2,512,1024]{2,3,1,0:T(8,128)} %get-tuple-element.111, f32[8,2,512]{2,1,0:T(2,128)S(1)} %bitcast.207, bf16[1024,8,64,1]{0,2,3,1:T(8,128)(2,1)S(1)} %bitcast.203, bf16[512,8,2,64]{0,3,2,1:T(8,128)(2,1)S(1)} %bitcast.190), kind=kOutput, calls=%fused_computation.7 | convolution fusion | flops 1098899456 | bytes 69271552 | tf_op jit(solution)/shard_map/qgrd,kgd->grqk/dot_general | solution.py:229
  561.0 15.3 %fusion.36 = bf16[8,64,1024]{2,1,0:T(8,128)(2,1)} fusion(f32[8,64,1024,1]{2,1,3,0:T(8,128)} %fusion.11, bf16[512,8,2,64]{0,3,2,1:T(8,128)(2,1)S(1)} %bitcast.191, f32[8,2,512,1024]{2,3,1,0:T(8,128)} %get-tuple-element.111, f32[8,2,512]{2,1,0:T(2,128)S(1)} %bitcast.208), kind=kOutput, calls=%fused_computation.90 | convolution fusion | flops 1091567616 | bytes 37781504 | tf_op jit(solution)/shard_map/grqk,qgrd->kgd/dot_general | solution.py:241
  580.0 28.0 %fusion.5 = bf16[8,2,512,1024]{2,3,1,0:T(8,128)(2,1)} fusion(f32[8,1024,512,2]{2,1,3,0:T(8,128)} %get-tuple-element.118, f32[8,2,512,1024]{2,3,1,0:T(8,128)} %get-tuple-element.111, f32[8,2,512]{2,1,0:T(2,128)S(1)} %get-tuple-element.117, f32[8,2,512]{2,1,0:T(2,128)S(1)} %bitcast.209), kind=kLoop, calls=%fused_computation.9 | loop fusion | flops 33554432 | bytes 83951616 | tf_op jit(solution)/shard_map/convert_element_type | solution.py:233
  620.2 27.5 %fusion.2 = bf16[8,2,512,1024]{2,3,1,0:T(8,128)(2,1)} fusion(f32[8,1024,512,2]{2,1,3,0:T(8,128)} %get-tuple-element.116, f32[8,2,512,1024]{2,3,1,0:T(8,128)} %get-tuple-element.109, f32[8,2,512]{2,1,0:T(2,128)S(1)} %get-tuple-element.115, f32[8,2,512]{2,1,0:T(2,128)S(1)} %bitcast.206), kind=kLoop, calls=%fused_computation.4 | loop fusion | flops 33554432 | bytes 83951616 | tf_op jit(solution)/shard_map/convert_element_type | solution.py:233
  647.7 12.9 %fusion.38 = f32[1024,8,64]{0,2,1:T(8,128)} fusion(f32[8,64,1024,1]{2,1,3,0:T(8,128)} %fusion.68, bf16[512,8,2,64]{0,3,2,1:T(8,128)(2,1)S(1)} %bitcast.197, bf16[8,2,512,1024]{2,3,1,0:T(8,128)(2,1)} %fusion.2), kind=kOutput, calls=%fused_computation.97 | convolution fusion | flops 1074790400 | bytes 22020096 | tf_op jit(solution)/shard_map/grqk,qgrd->kgd/dot_general | solution.py:238
  702.9 16.7 %convolution_convert_fusion.1 = bf16[1024,4608]{1,0:T(8,128)(2,1)} fusion(bf16[1024,1024]{0,1:T(8,128)(2,1)} %copy-done.31, bf16[1024,4608]{1,0:T(8,128)(2,1)} %get-tuple-element.66), kind=kOutput, calls=%fused_computation.34 | convolution fusion | flops 9668395008 | bytes 20971520 | tf_op jit(solution)/shard_map/dot_general | solution.py:63
  719.7 16.3 %convolution_convert_fusion = bf16[1024,4608]{1,0:T(8,128)(2,1)} fusion(bf16[1024,1024]{0,1:T(8,128)(2,1)} %copy-done.31, bf16[1024,4608]{1,0:T(8,128)(2,1)} %get-tuple-element.65), kind=kOutput, calls=%fused_computation.33 | convolution fusion | flops 9668395008 | bytes 20971520 | tf_op jit(solution)/shard_map/dot_general | solution.py:63
  736.6 16.6 %convolution_convert_fusion.2 = bf16[4608,1024]{1,0:T(8,128)(2,1)} fusion(bf16[1024,4608]{1,0:T(8,128)(2,1)} %get-tuple-element.67, bf16[1024,1024]{0,1:T(8,128)(2,1)} %copy.65, f32[1024]{0:T(1024)S(1)} %copy-done.52), kind=kOutput, calls=%fused_computation.35 | convolution fusion | flops 9671540736 | bytes 20975616 | tf_op jit(solution)/shard_map/dot_general | solution.py:63
  754.8 17.3 %reduce-scatter.8.cloned.1.call-done = bf16[256,1024]{1,0:T(8,128)(2,1)} async-done(((bf16[1024,1024]{1,0:T(8,128)(2,1)}), bf16[256,1024]{1,0:T(8,128)(2,1)}) %reduce-scatter.8.cloned.1.call-update) | async-done | bytes 524304 | tf_op jit(solution)/shard_map/reduce_scatter | solution.py:281
  772.1 98.0 %reduce-scatter.16.cloned.1.call-done = bf16[256,4608]{1,0:T(8,128)(2,1)} async-done(((bf16[1024,4608]{1,0:T(8,128)(2,1)}), bf16[256,4608]{1,0:T(8,128)(2,1)}) %reduce-scatter.16.cloned.1.call-update) | async-done | bytes 2359312 | tf_op jit(solution)/shard_map/reduce_scatter | solution.py:193
  870.2 98.1 %reduce-scatter.18.cloned.1.call-done = bf16[256,4608]{1,0:T(8,128)(2,1)} async-done(((bf16[1024,4608]{1,0:T(8,128)(2,1)}), bf16[256,4608]{1,0:T(8,128)(2,1)}) %reduce-scatter.18.cloned.1.call-update) | async-done | bytes 2359312 | tf_op jit(solution)/shard_map/reduce_scatter | solution.py:196
  968.3 98.0 %reduce-scatter.20.cloned.1.call-done = bf16[1152,1024]{1,0:T(8,128)(2,1)} async-done(((bf16[4608,1024]{1,0:T(8,128)(2,1)}), bf16[1152,1024]{1,0:T(8,128)(2,1)}) %reduce-scatter.20.cloned.1.call-update) | async-done | bytes 2359312 | tf_op jit(solution)/shard_map/reduce_scatter | solution.py:199
  1066.4 16.9 %multiply_convert_fusion.3 = bf16[1024,1024]{0,1:T(8,128)(2,1)} fusion(f32[1024,1024]{0,1:T(8,128)} %copy-done.8, f32[1024]{0:T(1024)S(1)} %copy-done.52, bf16[1024,4608]{1,0:T(8,128)(2,1)} %get-tuple-element.67, bf16[4608,1024]{1,0:T(8,128)(2,1)} %all-gather.22.cloned.1.call-done), kind=kOutput, calls=%fused_computation.72 | convolution fusion | flops 9666822144 | bytes 25169920 | tf_op jit(solution)/shard_map/dot_general | solution.py:59
  1105.5 15.8 %all-reduce.4 = (bf16[256]{0:T(256)(128)(2,1)S(1)}, bf16[32]{0:T(256)(128)(2,1)S(1)}, bf16[256]{0:T(256)(128)(2,1)S(1)}) all-reduce(bf16[256]{0:T(256)(128)(2,1)S(1)} %dynamic-slice.2, bf16[32]{0:T(256)(128)(2,1)S(1)} %dynamic-slice.4, bf16[256]{0:T(256)(128)(2,1)S(1)} %dynamic-slice.6), channel_id=1, replica_groups=mesh['shard'=4,'rep'=8] {'rep'}, use_global_device_ids=true, to_apply=%region_17.18 | all-reduce | flops 544 | bytes 2176 | tf_op jit(solution)/shard_map/psum | solution.py:309
  1132.8 119.3 %all-reduce.9.cloned.1.call-done = (bf16[256,1024]{1,0:T(8,128)(2,1)}, bf16[256,512]{1,0:T(8,128)(2,1)}, bf16[256,512]{1,0:T(8,128)(2,1)}, bf16[256,1024]{1,0:T(...) async-done(((bf16[256,1024]{1,0:T(8,128)(2,1)}, bf16[256,512]{1,0:T(8,128)(2,1)}, bf16[256,512]{1,0:T(8,128)(2,1)}, ...) | async-done | bytes 8650768 | tf_op jit(solution)/shard_map/psum | solution.py:310
  (252 shorter events, 191.2 us)
Async XLA Ops:
  7.2 46.2 %all-gather.12.cloned.1.call-start = ((), (), s32[]{:S(2)}) async-start(), calls=%async_computation.8 | async-start | bytes 1310720 | tf_op jit(solution)/shard_map/all_gather | solution.py:97
  7.9 59.9 %all-gather.10.cloned.1.call-start = ((), (), s32[]{:S(2)}) async-start(), calls=%async_computation.7 | async-start | bytes 1310720 | tf_op jit(solution)/shard_map/all_gather | solution.py:98
  8.7 96.3 %all-gather.14.cloned.1.call-start = ((), (), s32[]{:S(2)}) async-start(), calls=%async_computation.9 | async-start | bytes 2621440 | tf_op jit(solution)/shard_map/all_gather | solution.py:96
  9.4 188.8 %all-gather.16.cloned.1.call-start = ((), (), s32[]{:S(2)}) async-start(), calls=%async_computation.10 | async-start | bytes 2621440 | tf_op jit(solution)/shard_map/all_gather | solution.py:100
  10.0 230.1 %all-gather.20.cloned.1.call-start = ((), (), s32[]{:S(2)}) async-start(), calls=%async_computation.12 | async-start | bytes 11796480 | tf_op jit(solution)/shard_map/all_gather | solution.py:155
  10.6 327.6 %all-gather.18.cloned.1.call-start = ((), (), s32[]{:S(2)}) async-start(), calls=%async_computation.11 | async-start | bytes 11796480 | tf_op jit(solution)/shard_map/all_gather | solution.py:154
  11.2 425.2 %all-gather.22.cloned.1.call-start = ((), (), s32[]{:S(2)}) async-start(), calls=%async_computation.13 | async-start | bytes 11796480 | tf_op jit(solution)/shard_map/all_gather | solution.py:156
  11.9 742.8 %reduce-scatter.12.cloned.1.call-start = ((), (), s32[]{:S(2)}) async-start(), calls=%async_computation.16 | async-start | bytes 1310720 | tf_op jit(solution)/shard_map/reduce_scatter | solution.py:287
  26.7 30.0 %copy-start.56 = (f32[64]{0:T(128)}, f32[64]{0:T(128)S(1)}, u32[]{:S(2)}) copy-start(f32[64]{0:T(128)S(1)} %get-tuple-element.102) | copy-start | bytes 772
  26.7 83.2 %copy-start.54 = (f32[64]{0:T(128)}, f32[64]{0:T(128)S(1)}, u32[]{:S(2)}) copy-start(f32[64]{0:T(128)S(1)} %get-tuple-element.103) | copy-start | bytes 772
  42.5 62.5 %copy-start.47 = (f32[4,1,256]{2,1,0:T(1,128)}, f32[4,1,256]{2,1,0:T(1,128)S(1)}, u32[]{:S(2)}) copy-start(f32[4,1,256]{2,1,0:T(1,128)S(1)} %convert_element_type.226) | copy-start | bytes 12292
  47.5 57.5 %copy-start.2 = (bf16[1024,1024]{0,1:T(8,128)(2,1)}, bf16[1024,1024]{0,1:T(8,128)(2,1)S(1)}, u32[]{:S(2)}) copy-start(bf16[1024,1024]{0,1:T(8,128)(2,1)S(1)} %copy.61) | copy-start | bytes 6291460
  48.8 56.2 %copy-start.44 = (f32[1024]{0:T(1024)}, f32[1024]{0:T(1024)S(1)}, u32[]{:S(2)}) copy-start(f32[1024]{0:T(1024)S(1)} %get-tuple-element.97) | copy-start | bytes 12292
  53.3 57.7 %copy-start.24 = (f32[1024,32]{0,1:T(8,128)}, f32[1024,32]{0,1:T(8,128)S(1)}, u32[]{:S(2)}) copy-start(f32[1024,32]{0,1:T(8,128)S(1)} %get-tuple-element.94) | copy-start | bytes 393220
  53.3 57.7 %copy-start.26 = (f32[1024,32]{0,1:T(8,128)}, f32[1024,32]{0,1:T(8,128)S(1)}, u32[]{:S(2)}) copy-start(f32[1024,32]{0,1:T(8,128)S(1)} %get-tuple-element.95) | copy-start | bytes 393220
  58.3 96.5 %copy-start.10 = (bf16[1024,8,32]{0,2,1:T(8,128)(2,1)}, bf16[1024,8,32]{0,2,1:T(8,128)(2,1)S(1)}, u32[]{:S(2)}) copy-start(bf16[1024,8,32]{0,2,1:T(8,128)(2,1)S(1)} %get-tuple-element.80) | copy-start | bytes 1572868
  58.3 96.5 %copy-start.12 = (bf16[1024,8,32]{0,2,1:T(8,128)(2,1)}, bf16[1024,8,32]{0,2,1:T(8,128)(2,1)S(1)}, u32[]{:S(2)}) copy-start(bf16[1024,8,32]{0,2,1:T(8,128)(2,1)S(1)} %get-tuple-element.81) | copy-start | bytes 1572868
  112.5 42.3 %copy-start.14 = (bf16[512,16,64]{0,2,1:T(8,128)(2,1)}, bf16[512,16,64]{0,2,1:T(8,128)(2,1)S(1)}, u32[]{:S(2)}) copy-start(bf16[512,16,64]{0,2,1:T(8,128)(2,1)S(1)} %get-tuple-element.86) | copy-start | bytes 3145732
  205.5 34.6 %copy-start.31 = (bf16[1024,1024]{0,1:T(8,128)(2,1)}, bf16[1024,1024]{0,1:T(8,128)(2,1)S(1)}, u32[]{:S(2)}) copy-start(bf16[1024,1024]{0,1:T(8,128)(2,1)S(1)} %multiply_convert_fusion.4) | copy-start | bytes 6291460
  256.3 180.1 %copy-start.18 = (bf16[1024,1024]{0,1:T(8,128)(2,1)S(1)}, bf16[1024,1024]{0,1:T(8,128)(2,1)}, u32[]{:S(2)}) copy-start(bf16[1024,1024]{0,1:T(8,128)(2,1)} %copy.65) | copy-start | bytes 6291460
  256.3 180.1 %copy-start.51 = (f32[1024]{0:T(1024)S(1)}, f32[1024]{0:T(1024)}, u32[]{:S(2)}) copy-start(f32[1024]{0:T(1024)} %compare_convert_fusion) | copy-start | bytes 12292
  517.5 21.8 %copy-start.37 = (f32[2,8,512]{2,1,0:T(8,128)S(1)}, f32[2,8,512]{2,1,0:T(8,128)}, u32[]{:S(2)}) copy-start(f32[2,8,512]{2,1,0:T(8,128)} %log_add_fusion.1) | copy-start | bytes 98308
  579.9 174.9 %reduce-scatter.10.cloned.1.call-start = ((), (), s32[]{:S(2)}) async-start(), calls=%async_computation.15 | async-start | bytes 1310720 | tf_op jit(solution)/shard_map/reduce_scatter | solution.py:284
  580.0 28.0 %copy-start.15 = (bf16[512,16,64]{0,2,1:T(8,128)(2,1)S(1)}, bf16[512,16,64]{0,2,1:T(8,128)(2,1)}, u32[]{:S(2)}) copy-start(bf16[512,16,64]{0,2,1:T(8,128)(2,1)} %copy-done.14) | copy-start | bytes 3145732
  620.2 27.5 %copy-start.17 = (bf16[512,16,64]{0,2,1:T(8,128)(2,1)S(1)}, bf16[512,16,64]{0,2,1:T(8,128)(2,1)}, u32[]{:S(2)}) copy-start(bf16[512,16,64]{0,2,1:T(8,128)(2,1)} %copy-done.16) | copy-start | bytes 3145732
  666.6 88.2 %reduce-scatter.14.cloned.1.call-start = ((), (), s32[]{:S(2)}) async-start(), calls=%async_computation.17 | async-start | bytes 2621440 | tf_op jit(solution)/shard_map/reduce_scatter | solution.py:293
  673.4 98.8 %reduce-scatter.8.cloned.1.call-start = ((), (), s32[]{:S(2)}) async-start(), calls=%async_computation.14 | async-start | bytes 2621440 | tf_op jit(solution)/shard_map/reduce_scatter | solution.py:281
  702.7 167.5 %reduce-scatter.16.cloned.1.call-start = ((), (), s32[]{:S(2)}) async-start(), calls=%async_computation.18 | async-start | bytes 11796480 | tf_op jit(solution)/shard_map/reduce_scatter | solution.py:193
  719.6 248.7 %reduce-scatter.18.cloned.1.call-start = ((), (), s32[]{:S(2)}) async-start(), calls=%async_computation.19 | async-start | bytes 11796480 | tf_op jit(solution)/shard_map/reduce_scatter | solution.py:196
  736.0 330.4 %reduce-scatter.20.cloned.1.call-start = ((), (), s32[]{:S(2)}) async-start(), calls=%async_computation.20 | async-start | bytes 11796480 | tf_op jit(solution)/shard_map/reduce_scatter | solution.py:199
  753.2 499.0 %all-reduce.9.cloned.1.call-start = ((), (), s32[]{:S(2)}) async-start(), calls=%async_computation.21 | async-start | bytes 17301504 | tf_op jit(solution)/shard_map/psum | solution.py:310
  1092.6 30.3 %copy-start.50 = (f32[1024]{0:T(1024)S(1)}, f32[1024]{0:T(1024)}, u32[]{:S(2)}) copy-start(f32[1024]{0:T(1024)} %get-tuple-element.96) | copy-start | bytes 12292
  (48 other events, 293.7 us)
Sparse Core Ops, SparseCore 0:
  9.9 29.4 all-gather.11
  41.2 26.6 all-gather.9
  69.7 35.2 all-gather.13
  106.7 35.2 all-gather.15
  143.7 96.3 all-gather.19
  241.8 96.3 all-gather.17
  340.0 96.3 all-gather.21
  580.0 27.7 reduce-scatter.11
  666.7 28.3 reduce-scatter.9
  697.9 35.1 reduce-scatter.13
  736.9 35.1 reduce-scatter.7
  775.1 95.0 reduce-scatter.15
  873.3 94.9 reduce-scatter.17
  971.3 95.0 reduce-scatter.19
  1069.1 182.9 all-reduce.8
where the time goes:
time: 1280 us
  waiting for transfers between devices  676 us (53%)
  matrix products  379 us (30%)
  other arithmetic  125 us (10%)
  blocking collectives  51.4 us (4%)
  local copies, waits for them, and re-layouts  25.2 us (2%)
  between operations  17.1 us (1%)
    psum x1, waiting for transfers between devices, body(): lax.psum(share_query.astype(jnp.bfloat16), 'rep').astype(jnp.float32)  119 us
    reduce_scatter x1, waiting for transfers between devices, body(): lax.psum_scatter(grad_w_up.astype(jnp.bfloat16), 'shard', scatter_dimensi...  98.1 us
    reduce_scatter x1, waiting for transfers between devices, body(): lax.psum_scatter(grad_w_gate.astype(jnp.bfloat16), 'shard', scatter_dimen...  98 us
    reduce_scatter x1, waiting for transfers between devices, body(): lax.psum_scatter(grad_w_down.astype(jnp.bfloat16), 'shard', scatter_dimen...  98 us
    all_gather x1, waiting for transfers between devices, body(): lax.all_gather(w_gate, 'shard', axis=0, tiled=True)  81.8 us
    all_gather x1, waiting for transfers between devices, body(): lax.all_gather(w_down, 'shard', axis=0, tiled=True)  81.1 us
    dot_general x7, matrix products, matmul_cols(): lax.dot_general(left_mat, right_mat, (((1,), (1,)), ((), ())), preferred_...  73.2 us
    dot_general x7, matrix products, matmul_rows(): lax.dot_general(left_mat, right_mat, (((0,), (0,)), ((), ())), preferred_...  65.6 us
  transfers between devices with their start and end apart: 15, of which 10 were waited for; matrix products, arithmetic and copies ran while one was open for 28% of the time, Pallas kernels for 0%

commit v1 on v0

--- a/solution.py
+++ b/solution.py
@@ -307,7 +307,9 @@
         share_down,
     ) = (
         lax.psum(share_again.astype(jnp.bfloat16), "rep").astype(jnp.float32),
-        lax.psum(share_query.astype(jnp.bfloat16), "rep").astype(jnp.float32),
+        jnp.sum(lax.all_gather(share_query.astype(jnp.bfloat16), "rep"), axis=0).astype(
+            jnp.float32
+        ),
         lax.psum(share_key.astype(jnp.bfloat16), "rep").astype(jnp.float32),
         lax.psum(share_value.astype(jnp.bfloat16), "rep").astype(jnp.float32),
         lax.psum(share_qk.astype(jnp.bfloat16), "rep").astype(jnp.float32),

time: 1280 us -> 1320 us (1.031)
  waiting for transfers between devices: 676 us -> 710 us
    psum x1, waiting for transfers between devices: 119 us -> 152 us  [body(): lax.psum(share_key.astype(jnp.bfloat16), 'rep').astype(jnp.float32)]
    reduce_scatter x1, waiting for transfers between devices: 0.02 us -> 18 us  [body(): lax.psum_scatter(grad_w_out.astype(jnp.bfloat16), 'shard', scatter_dimens...]
    reduce_scatter x1, waiting for transfers between devices: 17.3 us -> 0.02 us  [body(): lax.psum_scatter(grad_w_query.astype(jnp.bfloat16), 'shard', scatter_dime...]
  transfers between devices with their start and end apart: 15 -> 16, of which waited for: 10 -> 10; matrix products, arithmetic and copies ran while one was open for 28% -> 24% of each run, Pallas kernels for 0% -> 0%
where the time goes in v1:
time: 1320 us
  waiting for transfers between devices  710 us (54%)
  matrix products  382 us (29%)
  other arithmetic  128 us (10%)
  blocking collectives  51.1 us (4%)
  local copies, waits for them, and re-layouts  27.8 us (2%)
  between operations  17.1 us (1%)
    psum x1, waiting for transfers between devices, body(): lax.psum(share_key.astype(jnp.bfloat16), 'rep').astype(jnp.float32)  152 us
    reduce_scatter x1, waiting for transfers between devices, body(): lax.psum_scatter(grad_w_up.astype(jnp.bfloat16), 'shard', scatter_dimensi...  98.1 us
    reduce_scatter x1, waiting for transfers between devices, body(): lax.psum_scatter(grad_w_down.astype(jnp.bfloat16), 'shard', scatter_dimen...  98 us
    reduce_scatter x1, waiting for transfers between devices, body(): lax.psum_scatter(grad_w_gate.astype(jnp.bfloat16), 'shard', scatter_dimen...  98 us
    all_gather x1, waiting for transfers between devices, body(): lax.all_gather(w_gate, 'shard', axis=0, tiled=True)  81.8 us
    all_gather x1, waiting for transfers between devices, body(): lax.all_gather(w_down, 'shard', axis=0, tiled=True)  81 us
    dot_general x7, matrix products, matmul_cols(): lax.dot_general(left_mat, right_mat, (((1,), (1,)), ((), ())), preferred_...  73.4 us
    dot_general x7, matrix products, matmul_rows(): lax.dot_general(left_mat, right_mat, (((0,), (0,)), ((), ())), preferred_...  65.6 us
  transfers between devices with their start and end apart: 16, of which 10 were waited for; matrix products, arithmetic and copies ran while one was open for 24% of the time, Pallas kernels for 0%

profile of v1, /device:TPU:0, one launch (start us, length us, event | category | flops | bytes accessed | tf_op | source)
XLA Modules:
  0.0 1316.8 jit_solution(3591209616796538809)
XLA Ops:
  71.4 33.6 %all-gather.16.cloned.1.call-done = bf16[1024,1024]{1,0:T(8,128)(2,1)} async-done(((bf16[256,1024]{1,0:T(8,128)(2,1)}), bf16[1024,1024]{1,0:T(8,128)(2,1)}) %all-gather.16.cloned.1.call-update) | async-done | bytes 2097168 | tf_op jit(solution)/shard_map/all_gather | solution.py:96
  112.6 13.5 %fusion.63 = (f32[8,2,512]{2,1,0:T(2,128)S(1)}, f32[8,2,512,1024]{2,3,1,0:T(8,128)}) fusion(bf16[512,8,2,64]{0,3,2,1:T(8,128)(2,1)S(1)} %bitcast.197, bf16[1024,8,32]{0,2,1:T(8,128)(2,1)S(1)} %get-tuple-element.80, bf16[1024,8,32]{0,2,1:T(8,128)(2,1)S(1)} %get-tuple-element.79, pred[512,1024]{0,1:T(8,128)(4,1)S(1)} %copy-done.22), kind=kOutput, calls=%fused_computation.153 | convolution fusion | flops 1100996608 | bytes 36208640 | tf_op jit(solution)/shard_map/qgrd,kgd->grqk/dot_general | solution.py:129
  126.1 14.0 %fusion.7 = f32[8,2,512]{2,1,0:T(2,128)S(1)} fusion(f32[8,2,512,1024]{2,3,1,0:T(8,128)} %get-tuple-element.108, f32[8,2,512]{2,1,0:T(2,128)S(1)} %get-tuple-element.107), kind=kLoop, calls=%fused_computation.19 | loop fusion | flops 16769024 | bytes 33619968 | tf_op jit(solution)/shard_map/reduce_sum | solution.py:142
  140.1 15.0 %fusion.44 = bf16[8,64,2,512]{3,1,2,0:T(8,128)(2,1)} fusion(bf16[1024,8,64,1]{0,2,3,1:T(8,128)(2,1)S(1)} %bitcast.201, f32[8,2,512,1024]{2,3,1,0:T(8,128)} %get-tuple-element.108, f32[8,2,512]{2,1,0:T(2,128)S(1)} %fusion.7, f32[8,2,512]{2,1,0:T(2,128)S(1)} %get-tuple-element.107), kind=kOutput, calls=%fused_computation.115 | convolution fusion | flops 1099431936 | bytes 35717120 | tf_op jit(solution)/shard_map/grqk,kgd->qgrd/dot_general | solution.py:146
  155.1 13.5 %fusion.64 = (f32[8,2,512]{2,1,0:T(2,128)S(1)}, f32[8,2,512,1024]{2,3,1,0:T(8,128)}) fusion(bf16[512,8,2,64]{0,3,2,1:T(8,128)(2,1)S(1)} %bitcast.195, bf16[1024,8,32]{0,2,1:T(8,128)(2,1)S(1)} %get-tuple-element.80, bf16[1024,8,32]{0,2,1:T(8,128)(2,1)S(1)} %get-tuple-element.79, pred[512,1024]{0,1:T(8,128)(4,1)S(1)} %copy-done.21), kind=kOutput, calls=%fused_computation.154 | convolution fusion | flops 1100996608 | bytes 36208640 | tf_op jit(solution)/shard_map/qgrd,kgd->grqk/dot_general | solution.py:129
  168.6 13.1 fusion.6
  181.8 16.5 %fusion.45 = bf16[8,64,2,512]{3,1,2,0:T(8,128)(2,1)} fusion(bf16[1024,8,64,1]{0,2,3,1:T(8,128)(2,1)S(1)} %bitcast.202, f32[8,2,512,1024]{2,3,1,0:T(8,128)} %get-tuple-element.110, f32[8,2,512]{2,1,0:T(2,128)S(1)} %fusion.6, f32[8,2,512]{2,1,0:T(2,128)S(1)} %get-tuple-element.109), kind=kOutput, calls=%fused_computation.116 | convolution fusion | flops 1099431936 | bytes 35717120 | tf_op jit(solution)/shard_map/grqk,kgd->qgrd/dot_general | solution.py:146
  205.6 34.5 %all-gather.22.cloned.1.call-done = bf16[1024,4608]{1,0:T(8,128)(2,1)} async-done(((bf16[256,4608]{1,0:T(8,128)(2,1)}), bf16[1024,4608]{1,0:T(8,128)(2,1)}) %all-gather.22.cloned.1.call-update) | async-done | bytes 9437200 | tf_op jit(solution)/shard_map/all_gather | solution.py:155
  240.1 16.2 %fusion.66 = f32[1024,4608]{1,0:T(8,128)} fusion(bf16[1024,1024]{0,1:T(8,128)(2,1)S(1)} %multiply_convert_fusion.4, bf16[1024,4608]{1,0:T(8,128)(2,1)} %all-gather.22.cloned.1.call-done), kind=kOutput, calls=%fused_computation.156 | convolution fusion | flops 9663676416 | bytes 30408704 | tf_op jit(solution)/shard_map/dot_general | solution.py:59
  256.3 81.8 %all-gather.20.cloned.1.call-done = bf16[1024,4608]{1,0:T(8,128)(2,1)} async-done(((bf16[256,4608]{1,0:T(8,128)(2,1)}), bf16[1024,4608]{1,0:T(8,128)(2,1)}) %all-gather.20.cloned.1.call-update) | async-done | bytes 9437200 | tf_op jit(solution)/shard_map/all_gather | solution.py:154
  338.2 17.2 %fusion.65 = f32[1024,4608]{1,0:T(8,128)} fusion(bf16[1024,1024]{0,1:T(8,128)(2,1)} %copy-done.33, bf16[1024,4608]{1,0:T(8,128)(2,1)} %all-gather.20.cloned.1.call-done), kind=kOutput, calls=%fused_computation.155 | convolution fusion | flops 9663676416 | bytes 30408704 | tf_op jit(solution)/shard_map/dot_general | solution.py:59
  355.4 81.0 %all-gather.24.cloned.1.call-done = bf16[4608,1024]{1,0:T(8,128)(2,1)} async-done(((bf16[1152,1024]{1,0:T(8,128)(2,1)}), bf16[4608,1024]{1,0:T(8,128)(2,1)}) %all-gather.24.cloned.1.call-update) | async-done | bytes 9437200 | tf_op jit(solution)/shard_map/all_gather | solution.py:156
  436.4 31.3 %multiply_convert_fusion = (bf16[1024,4608]{1,0:T(8,128)(2,1)}, bf16[1024,4608]{1,0:T(8,128)(2,1)}, bf16[1024,4608]{1,0:T(8,128)(2,1)}) fusion(f32[1024,4608]{1,0:T(8,128)} %fusion.65, f32[1024,4608]{1,0:T(8,128)} %fusion.66, bf16[4608,1024]{1,0:T(8,128)(2,1)} %all-gather.24.cloned.1.call-done, bf16[1024,1024]{0,1:T(8,128)(2,1)S(1)} %copy-done.19, ...), kind=kOutput, calls=%fused_computation.22 | convolution fusion | flops 9737601024 | bytes 77598720 | tf_op jit(solution)/shard_map/dot_general | solution.py:69
  467.7 14.6 %fusion.67 = f32[1024,1024]{0,1:T(8,128)S(1)} fusion(bf16[1024,4608]{1,0:T(8,128)(2,1)} %get-tuple-element.65, bf16[1024,4608]{1,0:T(8,128)(2,1)} %all-gather.20.cloned.1.call-done), kind=kOutput, calls=%fused_computation.157 | convolution fusion | flops 9663676416 | bytes 23068672 | tf_op jit(solution)/shard_map/dot_general | solution.py:69
  482.3 16.5 %multiply_reduce_fusion = (bf16[1024]{0:T(1024)(128)(2,1)}, f32[1024]{0:T(1024)S(1)}, f32[1024,1024]{0,1:T(8,128)S(1)}) fusion(f32[1024,1024]{0,1:T(8,128)S(1)} %copy-done.9, f32[1024]{0:T(1024)S(1)} %get-tuple-element.98, f32[1024]{0:T(1024)S(1)} %bitcast.225, f32[1024,1024]{0,1:T(8,128)S(1)} %fusion.67, bf16[1024,4608]{1,0:T(8,128)(2,1)} %get-tuple-element.64, ...), kind=kOutput, calls=%fused_computation.65 | convolution fusion | flops 9671014400 | bytes 31471616 | tf_op jit(solution)/shard_map/dot_general | solution.py:69
  504.3 21.8 %fusion.3 = (f32[8,2,512]{2,1,0:T(2,128)S(1)}, f32[8,1024,512,2]{2,1,3,0:T(8,128)}) fusion(f32[8,2,512,1024]{2,3,1,0:T(8,128)} %get-tuple-element.110, f32[8,2,512]{2,1,0:T(2,128)S(1)} %bitcast.206, bf16[1024,8,64,1]{0,2,3,1:T(8,128)(2,1)S(1)} %bitcast.203, bf16[512,8,2,64]{0,3,2,1:T(8,128)(2,1)S(1)} %bitcast.191), kind=kOutput, calls=%fused_computation.7 | convolution fusion | flops 1098899456 | bytes 69271552 | tf_op jit(solution)/shard_map/qgrd,kgd->grqk/dot_general | solution.py:229
  526.2 27.6 %fusion.5 = bf16[8,2,512,1024]{2,3,1,0:T(8,128)(2,1)} fusion(f32[8,1024,512,2]{2,1,3,0:T(8,128)} %get-tuple-element.117, f32[8,2,512,1024]{2,3,1,0:T(8,128)} %get-tuple-element.110, f32[8,2,512]{2,1,0:T(2,128)S(1)} %get-tuple-element.116, f32[8,2,512]{2,1,0:T(2,128)S(1)} %bitcast.207), kind=kLoop, calls=%fused_computation.9 | loop fusion | flops 33554432 | bytes 83951616 | tf_op jit(solution)/shard_map/convert_element_type | solution.py:233
  564.0 22.0 %fusion = (f32[8,2,512]{2,1,0:T(2,128)S(1)}, f32[8,1024,512,2]{2,1,3,0:T(8,128)}) fusion(f32[8,2,512,1024]{2,3,1,0:T(8,128)} %get-tuple-element.108, f32[8,2,512]{2,1,0:T(2,128)S(1)} %bitcast.209, bf16[1024,8,64,1]{0,2,3,1:T(8,128)(2,1)S(1)} %bitcast.204, bf16[512,8,2,64]{0,3,2,1:T(8,128)(2,1)S(1)} %bitcast.193), kind=kOutput, calls=%fused_computation.2 | convolution fusion | flops 1098899456 | bytes 69271552 | tf_op jit(solution)/shard_map/qgrd,kgd->grqk/dot_general | solution.py:229
  586.0 27.4 %fusion.2 = bf16[8,2,512,1024]{2,3,1,0:T(8,128)(2,1)} fusion(f32[8,1024,512,2]{2,1,3,0:T(8,128)} %get-tuple-element.115, f32[8,2,512,1024]{2,3,1,0:T(8,128)} %get-tuple-element.108, f32[8,2,512]{2,1,0:T(2,128)S(1)} %get-tuple-element.114, f32[8,2,512]{2,1,0:T(2,128)S(1)} %bitcast.210), kind=kLoop, calls=%fused_computation.4 | loop fusion | flops 33554432 | bytes 83951616 | tf_op jit(solution)/shard_map/convert_element_type | solution.py:233
  634.8 15.5 %fusion.11 = f32[8,64,1024,1]{2,1,3,0:T(8,128)} fusion(bf16[512,8,2,64]{0,3,2,1:T(8,128)(2,1)} %bitcast.194, f32[8,2,512,1024]{2,3,1,0:T(8,128)} %get-tuple-element.108, f32[8,2,512]{2,1,0:T(2,128)S(1)} %bitcast.211), kind=kOutput, calls=%fused_computation.27 | convolution fusion | flops 1090519040 | bytes 36732928 | tf_op jit(solution)/shard_map/grqk,qgrd->kgd/dot_general | solution.py:241
  650.3 15.6 %fusion.36 = bf16[8,64,1024]{2,1,0:T(8,128)(2,1)} fusion(f32[8,64,1024,1]{2,1,3,0:T(8,128)} %fusion.11, bf16[512,8,2,64]{0,3,2,1:T(8,128)(2,1)S(1)} %bitcast.192, f32[8,2,512,1024]{2,3,1,0:T(8,128)} %get-tuple-element.110, f32[8,2,512]{2,1,0:T(2,128)S(1)} %bitcast.208), kind=kOutput, calls=%fused_computation.90 | convolution fusion | flops 1091567616 | bytes 37781504 | tf_op jit(solution)/shard_map/grqk,qgrd->kgd/dot_general | solution.py:241
  682.2 13.3 %fusion.38 = f32[1024,8,64]{0,2,1:T(8,128)} fusion(f32[8,64,1024,1]{2,1,3,0:T(8,128)} %fusion.68, bf16[512,8,2,64]{0,3,2,1:T(8,128)(2,1)} %bitcast.198, bf16[8,2,512,1024]{2,3,1,0:T(8,128)(2,1)} %fusion.2), kind=kOutput, calls=%fused_computation.97 | convolution fusion | flops 1074790400 | bytes 22020096 | tf_op jit(solution)/shard_map/grqk,qgrd->kgd/dot_general | solution.py:238
  708.4 16.3 %convolution_convert_fusion.1 = bf16[1024,4608]{1,0:T(8,128)(2,1)} fusion(bf16[1024,1024]{0,1:T(8,128)(2,1)} %copy-done.33, bf16[1024,4608]{1,0:T(8,128)(2,1)} %get-tuple-element.65), kind=kOutput, calls=%fused_computation.34 | convolution fusion | flops 9668395008 | bytes 20971520 | tf_op jit(solution)/shard_map/dot_general | solution.py:63
  725.0 16.4 %convolution_convert_fusion = bf16[1024,4608]{1,0:T(8,128)(2,1)} fusion(bf16[1024,1024]{0,1:T(8,128)(2,1)} %copy-done.33, bf16[1024,4608]{1,0:T(8,128)(2,1)} %get-tuple-element.64), kind=kOutput, calls=%fused_computation.33 | convolution fusion | flops 9668395008 | bytes 20971520 | tf_op jit(solution)/shard_map/dot_general | solution.py:63
  742.1 16.6 %convolution_convert_fusion.2 = bf16[4608,1024]{1,0:T(8,128)(2,1)} fusion(bf16[1024,4608]{1,0:T(8,128)(2,1)} %get-tuple-element.66, bf16[1024,1024]{0,1:T(8,128)(2,1)} %copy.65, f32[1024]{0:T(1024)S(1)} %copy-done.54), kind=kOutput, calls=%fused_computation.35 | convolution fusion | flops 9671540736 | bytes 20975616 | tf_op jit(solution)/shard_map/dot_general | solution.py:63
  760.9 18.0 %reduce-scatter.14.cloned.1.call-done = bf16[256,1024]{1,0:T(8,128)(2,1)} async-done(((bf16[1024,1024]{1,0:T(8,128)(2,1)}), bf16[256,1024]{1,0:T(8,128)(2,1)}) %reduce-scatter.14.cloned.1.call-update) | async-done | bytes 524304 | tf_op jit(solution)/shard_map/reduce_scatter | solution.py:293
  778.9 98.0 %reduce-scatter.16.cloned.1.call-done = bf16[256,4608]{1,0:T(8,128)(2,1)} async-done(((bf16[1024,4608]{1,0:T(8,128)(2,1)}), bf16[256,4608]{1,0:T(8,128)(2,1)}) %reduce-scatter.16.cloned.1.call-update) | async-done | bytes 2359312 | tf_op jit(solution)/shard_map/reduce_scatter | solution.py:193
  876.9 98.1 %reduce-scatter.18.cloned.1.call-done = bf16[256,4608]{1,0:T(8,128)(2,1)} async-done(((bf16[1024,4608]{1,0:T(8,128)(2,1)}), bf16[256,4608]{1,0:T(8,128)(2,1)}) %reduce-scatter.18.cloned.1.call-update) | async-done | bytes 2359312 | tf_op jit(solution)/shard_map/reduce_scatter | solution.py:196
  975.1 98.0 %reduce-scatter.20.cloned.1.call-done = bf16[1152,1024]{1,0:T(8,128)(2,1)} async-done(((bf16[4608,1024]{1,0:T(8,128)(2,1)}), bf16[1152,1024]{1,0:T(8,128)(2,1)}) %reduce-scatter.20.cloned.1.call-update) | async-done | bytes 2359312 | tf_op jit(solution)/shard_map/reduce_scatter | solution.py:199
  1073.1 16.9 %multiply_convert_fusion.3 = bf16[1024,1024]{0,1:T(8,128)(2,1)} fusion(f32[1024,1024]{0,1:T(8,128)} %copy-done.8, f32[1024]{0:T(1024)S(1)} %copy-done.54, bf16[1024,4608]{1,0:T(8,128)(2,1)} %get-tuple-element.66, bf16[4608,1024]{1,0:T(8,128)(2,1)} %all-gather.24.cloned.1.call-done), kind=kOutput, calls=%fused_computation.72 | convolution fusion | flops 9666822144 | bytes 25169920 | tf_op jit(solution)/shard_map/dot_general | solution.py:59
  1112.2 15.5 %all-reduce.4 = (bf16[256]{0:T(256)(128)(2,1)S(1)}, bf16[32]{0:T(256)(128)(2,1)S(1)}, bf16[256]{0:T(256)(128)(2,1)S(1)}) all-reduce(bf16[256]{0:T(256)(128)(2,1)S(1)} %dynamic-slice.2, bf16[32]{0:T(256)(128)(2,1)S(1)} %dynamic-slice.4, bf16[256]{0:T(256)(128)(2,1)S(1)} %dynamic-slice.6), channel_id=1, replica_groups=mesh['shard'=4,'rep'=8] {'rep'}, use_global_device_ids=true, to_apply=%region_17.18 | all-reduce | flops 544 | bytes 2176 | tf_op jit(solution)/shard_map/psum | solution.py:309
  1143.4 152.4 %all-reduce.9.cloned.1.call-done = (bf16[256,512]{1,0:T(8,128)(2,1)}, bf16[256,512]{1,0:T(8,128)(2,1)}, bf16[256,1024]{1,0:T(8,128)(2,1)}, bf16[256,4608]{1,0:T(...) async-done(((bf16[256,512]{1,0:T(8,128)(2,1)}, bf16[256,512]{1,0:T(8,128)(2,1)}, bf16[256,1024]{1,0:T(8,128)(2,1)}, bf16[256,4608]{1,0:T(8,128)(2,1)}, ...) | async-done | bytes 8126480 | tf_op jit(solution)/shard_map/psum | solution.py:313
  (260 shorter events, 197.9 us)
Async XLA Ops:
  7.2 46.9 %all-gather.14.cloned.1.call-start = ((), (), s32[]{:S(2)}) async-start(), calls=%async_computation.8 | async-start | bytes 1310720 | tf_op jit(solution)/shard_map/all_gather | solution.py:97
  7.9 59.9 %all-gather.12.cloned.1.call-start = ((), (), s32[]{:S(2)}) async-start(), calls=%async_computation.7 | async-start | bytes 1310720 | tf_op jit(solution)/shard_map/all_gather | solution.py:98
  8.7 96.3 %all-gather.16.cloned.1.call-start = ((), (), s32[]{:S(2)}) async-start(), calls=%async_computation.9 | async-start | bytes 2621440 | tf_op jit(solution)/shard_map/all_gather | solution.py:96
  9.4 188.9 %all-gather.18.cloned.1.call-start = ((), (), s32[]{:S(2)}) async-start(), calls=%async_computation.10 | async-start | bytes 2621440 | tf_op jit(solution)/shard_map/all_gather | solution.py:100
  10.0 230.1 %all-gather.22.cloned.1.call-start = ((), (), s32[]{:S(2)}) async-start(), calls=%async_computation.12 | async-start | bytes 11796480 | tf_op jit(solution)/shard_map/all_gather | solution.py:155
  10.6 327.6 %all-gather.20.cloned.1.call-start = ((), (), s32[]{:S(2)}) async-start(), calls=%async_computation.11 | async-start | bytes 11796480 | tf_op jit(solution)/shard_map/all_gather | solution.py:154
  11.2 425.2 %all-gather.24.cloned.1.call-start = ((), (), s32[]{:S(2)}) async-start(), calls=%async_computation.13 | async-start | bytes 11796480 | tf_op jit(solution)/shard_map/all_gather | solution.py:156
  11.9 746.8 %reduce-scatter.8.cloned.1.call-start = ((), (), s32[]{:S(2)}) async-start(), calls=%async_computation.14 | async-start | bytes 2621440 | tf_op jit(solution)/shard_map/reduce_scatter | solution.py:281
  26.7 30.7 %copy-start.56 = (f32[64]{0:T(128)}, f32[64]{0:T(128)S(1)}, u32[]{:S(2)}) copy-start(f32[64]{0:T(128)S(1)} %get-tuple-element.101) | copy-start | bytes 772
  26.7 83.2 %copy-start.58 = (f32[64]{0:T(128)}, f32[64]{0:T(128)S(1)}, u32[]{:S(2)}) copy-start(f32[64]{0:T(128)S(1)} %get-tuple-element.102) | copy-start | bytes 772
  42.5 62.5 %copy-start.47 = (f32[4,1,256]{2,1,0:T(1,128)}, f32[4,1,256]{2,1,0:T(1,128)S(1)}, u32[]{:S(2)}) copy-start(f32[4,1,256]{2,1,0:T(1,128)S(1)} %convert_element_type.228) | copy-start | bytes 12292
  48.3 56.7 %copy-start.2 = (bf16[1024,1024]{0,1:T(8,128)(2,1)}, bf16[1024,1024]{0,1:T(8,128)(2,1)S(1)}, u32[]{:S(2)}) copy-start(bf16[1024,1024]{0,1:T(8,128)(2,1)S(1)} %copy.61) | copy-start | bytes 6291460
  49.6 55.4 %copy-start.44 = (f32[1024]{0:T(1024)}, f32[1024]{0:T(1024)S(1)}, u32[]{:S(2)}) copy-start(f32[1024]{0:T(1024)S(1)} %get-tuple-element.96) | copy-start | bytes 12292
  54.1 56.9 %copy-start.26 = (f32[1024,32]{0,1:T(8,128)}, f32[1024,32]{0,1:T(8,128)S(1)}, u32[]{:S(2)}) copy-start(f32[1024,32]{0,1:T(8,128)S(1)} %get-tuple-element.93) | copy-start | bytes 393220
  54.1 56.9 %copy-start.28 = (f32[1024,32]{0,1:T(8,128)}, f32[1024,32]{0,1:T(8,128)S(1)}, u32[]{:S(2)}) copy-start(f32[1024,32]{0,1:T(8,128)S(1)} %get-tuple-element.94) | copy-start | bytes 393220
  59.0 96.1 %copy-start.10 = (bf16[1024,8,32]{0,2,1:T(8,128)(2,1)}, bf16[1024,8,32]{0,2,1:T(8,128)(2,1)S(1)}, u32[]{:S(2)}) copy-start(bf16[1024,8,32]{0,2,1:T(8,128)(2,1)S(1)} %get-tuple-element.79) | copy-start | bytes 1572868
  59.0 96.0 %copy-start.12 = (bf16[1024,8,32]{0,2,1:T(8,128)(2,1)}, bf16[1024,8,32]{0,2,1:T(8,128)(2,1)S(1)}, u32[]{:S(2)}) copy-start(bf16[1024,8,32]{0,2,1:T(8,128)(2,1)S(1)} %get-tuple-element.80) | copy-start | bytes 1572868
  112.5 42.5 %copy-start.15 = (bf16[512,16,64]{0,2,1:T(8,128)(2,1)}, bf16[512,16,64]{0,2,1:T(8,128)(2,1)S(1)}, u32[]{:S(2)}) copy-start(bf16[512,16,64]{0,2,1:T(8,128)(2,1)S(1)} %get-tuple-element.85) | copy-start | bytes 3145732
  205.6 34.5 %copy-start.33 = (bf16[1024,1024]{0,1:T(8,128)(2,1)}, bf16[1024,1024]{0,1:T(8,128)(2,1)S(1)}, u32[]{:S(2)}) copy-start(bf16[1024,1024]{0,1:T(8,128)(2,1)S(1)} %multiply_convert_fusion.4) | copy-start | bytes 6291460
  256.3 180.1 %copy-start.19 = (bf16[1024,1024]{0,1:T(8,128)(2,1)S(1)}, bf16[1024,1024]{0,1:T(8,128)(2,1)}, u32[]{:S(2)}) copy-start(bf16[1024,1024]{0,1:T(8,128)(2,1)} %copy.65) | copy-start | bytes 6291460
  256.3 180.1 %copy-start.53 = (f32[1024]{0:T(1024)S(1)}, f32[1024]{0:T(1024)}, u32[]{:S(2)}) copy-start(f32[1024]{0:T(1024)} %compare_convert_fusion) | copy-start | bytes 12292
  503.0 61.0 %copy-start.14 = (bf16[512,1024]{0,1:T(8,128)(2,1)}, bf16[512,1024]{0,1:T(8,128)(2,1)S(1)}, u32[]{:S(2)}) copy-start(bf16[512,1024]{0,1:T(8,128)(2,1)S(1)} %get-tuple-element.84) | copy-start | bytes 3145732
  526.1 27.7 %copy-start.11 = (bf16[1024,8,32]{0,2,1:T(8,128)(2,1)S(1)}, bf16[1024,8,32]{0,2,1:T(8,128)(2,1)}, u32[]{:S(2)}) copy-start(bf16[1024,8,32]{0,2,1:T(8,128)(2,1)} %copy-done.10) | copy-start | bytes 1572868
  634.7 126.1 %reduce-scatter.12.cloned.1.call-start = ((), (), s32[]{:S(2)}) async-start(), calls=%async_computation.16 | async-start | bytes 1310720 | tf_op jit(solution)/shard_map/reduce_scatter | solution.py:287
  681.7 79.1 %reduce-scatter.10.cloned.1.call-start = ((), (), s32[]{:S(2)}) async-start(), calls=%async_computation.15 | async-start | bytes 1310720 | tf_op jit(solution)/shard_map/reduce_scatter | solution.py:284
  701.6 77.3 %reduce-scatter.14.cloned.1.call-start = ((), (), s32[]{:S(2)}) async-start(), calls=%async_computation.17 | async-start | bytes 2621440 | tf_op jit(solution)/shard_map/reduce_scatter | solution.py:293
  708.4 168.5 %reduce-scatter.16.cloned.1.call-start = ((), (), s32[]{:S(2)}) async-start(), calls=%async_computation.18 | async-start | bytes 11796480 | tf_op jit(solution)/shard_map/reduce_scatter | solution.py:193
  724.8 250.3 %reduce-scatter.18.cloned.1.call-start = ((), (), s32[]{:S(2)}) async-start(), calls=%async_computation.19 | async-start | bytes 11796480 | tf_op jit(solution)/shard_map/reduce_scatter | solution.py:196
  741.4 331.7 %reduce-scatter.20.cloned.1.call-start = ((), (), s32[]{:S(2)}) async-start(), calls=%async_computation.20 | async-start | bytes 11796480 | tf_op jit(solution)/shard_map/reduce_scatter | solution.py:199
  758.7 380.5 %all-gather.26.cloned.1.call-start = ((), (), s32[]{:S(2)}) async-start(), calls=%async_computation.21 | async-start | bytes 4718592 | tf_op jit(solution)/shard_map/all_gather | solution.py:310
  759.2 536.5 %all-reduce.9.cloned.1.call-start = ((), (), s32[]{:S(2)}) async-start(), calls=%async_computation.22 | async-start | bytes 16252928 | tf_op jit(solution)/shard_map/psum | solution.py:313
  1099.3 30.0 %copy-start.50 = (f32[1024]{0:T(1024)S(1)}, f32[1024]{0:T(1024)}, u32[]{:S(2)}) copy-start(f32[1024]{0:T(1024)} %get-tuple-element.95) | copy-start | bytes 12292
  (51 other events, 266.1 us)
Sparse Core Ops, SparseCore 0:
  9.9 29.4 all-gather.13
  41.2 26.6 all-gather.11
  69.7 35.2 all-gather.15
  106.7 35.2 all-gather.17
  143.7 96.3 all-gather.21
  241.8 96.3 all-gather.19
  340.0 96.3 all-gather.23
  634.8 35.1 reduce-scatter.7
  681.9 27.4 reduce-scatter.11
  712.1 27.7 reduce-scatter.9
  743.7 35.1 reduce-scatter.13
  781.8 95.0 reduce-scatter.15
  880.0 95.0 reduce-scatter.17
  978.0 95.0 reduce-scatter.19
  1074.5 47.2 all-gather.25
  1124.6 171.1 all-reduce.8
